TPU v7x, 32 devices: a whole 2x2x4 slice. The times are simulated.
32 devices in a mesh: replica: 4 (over z), shard: 8 (over y, x, core).
Axes of the slice: x: 2, y: 2, z: 4, core: 2. Of those that a mesh axis runs over, the one named last changes fastest.
Arguments:
- activations: bfloat16 [4, 2048, 4096], P('replica', 'shard'), may hold values from -6 to 6
- head_inputs: bfloat16 [4, 2048, 4096], P('replica', 'shard'), may hold values from -6 to 6
- out_cotangent: bfloat16 [4, 2048, 4096], P('replica', 'shard'), may hold values from -6 to 6
- episode_spans: int32 [4, 4], P('replica'), may hold values from 1 to 8, 16 in all within a row
- last_valid: int32 [4, 4], P('replica'), may hold values from 1 to 128, as said below
- mixer_weight: bfloat16 [4096, 256], P('shard'), may hold values from -0.09375 to 0.09375
- step_weight: bfloat16 [4096, 64], P('shard'), may hold values from -0.09375 to 0.09375
- decay_log: float32 [64], replicated, may hold values from 0 to 2.77
- step_bias: float32 [64], replicated, may hold values from -6.9 to -2.3
- skip_gain: float32 [64], replicated, may hold values from -3 to 3
Outputs:
- inputs_grad: bfloat16 [4, 2048, 4096], P('replica', 'shard')
- activations_grad: bfloat16 [4, 2048, 4096], P('replica', 'shard')
- mixer_grad: float32 [4096, 256], P('shard')
- step_grad: float32 [4096, 64], P('shard')
- decay_grad: float32 [64], replicated
- bias_grad: float32 [64], replicated
- skip_grad: float32 [64], replicated
Inputs may be any that keep to these rules, and one draw needn't show every extreme that they name: `episode_spans`: each group's 4 episode lengths, in spans of 128 tokens, add up to 16. `last_valid`: tokens after the valid ones in an episode's last span are padding.
All inputs are finite; a program needn't handle non-finite values.
Results may differ from a plain program's by a relative error of at most 0.018.
Values may be sent and summed in bfloat16 or wider, within the bound.
A program may use at most 320 MiB of HBM per device.

v0:
```python
import jax
import jax.numpy as jnp
from jax import lax
from jax.sharding import PartitionSpec as P

STATE = 128
SPAN = 128


def entering_2(value, axis, combine, identity, reverse):
    count, index = (lax.axis_size(axis), lax.axis_index(axis))
    everything = jax.tree.map(
        lambda part, kind: lax.all_gather(part.astype(kind), axis),
        value,
        jax.tree.map(lambda a: jnp.bfloat16 if a.dtype == jnp.float32 else a.dtype, value),
    )
    start = jax.tree.map(
        lambda part, zero: jnp.broadcast_to(jnp.asarray(zero, part.dtype), part.shape),
        value,
        identity,
    )

    def step(k, before):
        at = count - 1 - k if reverse else k
        reached = at > index if reverse else at < index
        new = combine(
            before, jax.tree.map(lambda part, own: part[at].astype(own.dtype), everything, value)
        )
        return jax.tree.map(lambda a, b: jnp.where(reached, a, b), new, before)

    return lax.fori_loop(0, count, step, start)


def span_layout(episode_spans, last_valid, first_span, span_count):
    span_ids = first_span + jnp.arange(span_count, dtype=jnp.int32)
    starts = jnp.cumsum(episode_spans) - episode_spans
    finals = starts + episode_spans - 1
    resets = jnp.any(span_ids[:, None] == starts[None, :], axis=1)
    final_hit = span_ids[:, None] == finals[None, :]
    valid_count = jnp.sum(jnp.where(final_hit, last_valid[None, :] - SPAN, 0), axis=1) + SPAN
    offsets = jnp.arange(SPAN, dtype=jnp.int32)
    valid_mask = jnp.where(offsets[None, :] < valid_count[:, None], 1.0, 0.0).astype(jnp.float32)
    keep_flag = jnp.where(resets, 0.0, 1.0).astype(jnp.float32)
    return (valid_mask, keep_flag)


def span_end(mixers, step_sizes, inputs, decay_log):
    length = inputs.shape[0]
    head_count = decay_log.shape[0]
    per_head = inputs.reshape(length, head_count, -1)
    cumulative = jnp.cumsum(step_sizes * (-jnp.exp(decay_log))[None, :], axis=0)
    weights = jnp.exp(cumulative[-1][None, :] - cumulative) * step_sizes
    weighted = (per_head * weights[:, :, None]).astype(jnp.bfloat16)
    end_state = jnp.einsum(
        "lhp,ln->hpn", weighted, mixers[:, :STATE], preferred_element_type=jnp.float32
    )
    return (jnp.exp(cumulative[-1]), end_state)


def span_out(mixers, step_sizes, inputs, entering, decay_log, skip_gain, valid_mask):
    length = inputs.shape[0]
    head_count = decay_log.shape[0]
    per_head = inputs.reshape(length, head_count, -1)
    input_map = mixers[:, :STATE]
    output_map = mixers[:, STATE:]
    cumulative = jnp.cumsum(step_sizes * (-jnp.exp(decay_log))[None, :], axis=0)
    scores = lax.dot_general(
        output_map, input_map, (((1,), (1,)), ((), ())), preferred_element_type=jnp.float32
    )
    by_head = cumulative.T
    causal = jnp.arange(length)[:, None] >= jnp.arange(length)[None, :]
    gaps = jnp.where(causal[None], by_head[:, :, None] - by_head[:, None, :], -jnp.inf)
    mixing = jnp.exp(gaps) * scores[None] * step_sizes.T[:, None, :]
    mixing = mixing.astype(jnp.bfloat16)
    inner = jnp.einsum("hls,shp->lhp", mixing, per_head, preferred_element_type=jnp.float32)
    entering_low = entering.astype(jnp.bfloat16)
    carried = jnp.einsum(
        "ln,hpn->lhp", output_map, entering_low, preferred_element_type=jnp.float32
    )
    carried = carried * jnp.exp(cumulative)[:, :, None]
    total = inner + carried + skip_gain[None, :, None] * per_head
    return total.reshape(length, -1) * valid_mask[:, None]


def chain_step(earlier, later):
    return (earlier[0] * later[0], later[1] + later[0][:, None, None] * earlier[1])


def shards(
    activations,
    head_inputs,
    out_cotangent,
    episode_spans,
    last_valid,
    mixer_weight,
    step_weight,
    decay_log,
    step_bias,
    skip_gain,
):
    token_rows = activations[0]
    inputs_here = head_inputs[0]
    tokens_here = token_rows.shape[0]
    span_count = tokens_here // SPAN
    head_count = decay_log.shape[0]
    first_span = lax.axis_index("shard") * span_count
    valid_mask, keep_flag = span_layout(episode_spans[0], last_valid[0], first_span, span_count)
    flat_mask = valid_mask.reshape(-1)
    joined = jnp.concatenate([mixer_weight, step_weight], axis=1)
    gathered = lax.all_gather(joined, "shard", axis=0, tiled=True)
    projected = jnp.dot(token_rows, gathered, preferred_element_type=jnp.float32)
    mixers = projected[:, : 2 * STATE].astype(jnp.bfloat16)
    raw_steps = projected[:, 2 * STATE :] + step_bias[None, :]

    def end_part(mixers, raw_steps, inputs, decay_log):
        step_sizes = jax.nn.softplus(raw_steps) * flat_mask[:, None]
        return lax.map(
            lambda pieces: span_end(pieces[0], pieces[1], pieces[2], decay_log),
            (
                mixers.reshape(span_count, SPAN, -1),
                step_sizes.reshape(span_count, SPAN, -1),
                inputs.reshape(span_count, SPAN, -1),
            ),
        )

    def out_part(mixers, raw_steps, inputs, entering, decay_log, skip_gain):
        step_sizes = jax.nn.softplus(raw_steps) * flat_mask[:, None]
        return lax.map(
            lambda pieces: span_out(
                pieces[0], pieces[1], pieces[2], pieces[3], decay_log, skip_gain, pieces[4]
            ),
            (
                mixers.reshape(span_count, SPAN, -1),
                step_sizes.reshape(span_count, SPAN, -1),
                inputs.reshape(span_count, SPAN, -1),
                entering,
                valid_mask,
            ),
        )

    (decays, states), end_pull = jax.vjp(end_part, mixers, raw_steps, inputs_here, decay_log)
    factors = decays * keep_flag[:, None]
    identity_pair = (jnp.ones((head_count,), jnp.float32), jnp.zeros(states.shape[1:], jnp.float32))

    def fold_spans(running, pieces):
        return (chain_step(running, pieces), None)

    local_total, _ = lax.scan(fold_spans, identity_pair, (factors, states))
    before_dev = entering_2(local_total, "shard", chain_step, identity_pair, False)

    def pass_forward(carry, pieces):
        entering = carry * pieces[2]
        return (pieces[0][:, None, None] * carry + pieces[1], entering)

    _, entering = lax.scan(pass_forward, before_dev[1], (factors, states, keep_flag))
    _, out_pull = jax.vjp(out_part, mixers, raw_steps, inputs_here, entering, decay_log, skip_gain)
    cotangent = out_cotangent[0].astype(jnp.float32).reshape(span_count, SPAN, -1)
    mixer_first, raw_first, input_first, enter_grad, decay_first, skip_local = out_pull(cotangent)
    local_terms = enter_grad * keep_flag[:, None, None, None]
    back_total, _ = lax.scan(fold_spans, identity_pair, (factors, local_terms), reverse=True)
    after_dev = entering_2(back_total, "shard", chain_step, identity_pair, True)

    def pass_back(carry, pieces):
        return (pieces[0][:, None, None] * carry + pieces[1], carry)

    _, ends_grad = lax.scan(pass_back, after_dev[1], (factors, local_terms), reverse=True)
    decay_cot = jnp.sum(ends_grad * entering, axis=(2, 3))
    mixer_second, raw_second, input_second, decay_second = end_pull((decay_cot, ends_grad))
    mixer_cot = mixer_first + mixer_second
    raw_cot = raw_first + raw_second
    input_grad = input_first + input_second
    joined_cot = jnp.concatenate([mixer_cot, raw_cot.astype(jnp.bfloat16)], axis=1)
    back_rows = lax.dot_general(
        joined_cot, gathered, (((1,), (1,)), ((), ())), preferred_element_type=jnp.float32
    )
    grads_local = lax.dot_general(
        token_rows, joined_cot, (((0,), (0,)), ((), ())), preferred_element_type=jnp.float32
    )
    shared = lax.psum_scatter(
        grads_local.astype(jnp.bfloat16), "shard", scatter_dimension=0, tiled=True
    )
    summed = lax.psum(shared, "replica").astype(jnp.float32)
    small = lax.psum(
        (decay_first + decay_second, jnp.sum(raw_cot, axis=0), skip_local), ("replica", "shard")
    )
    return (
        input_grad[None],
        back_rows.astype(jnp.bfloat16)[None],
        summed[:, : 2 * STATE],
        summed[:, 2 * STATE :],
        small[0],
        small[1],
        small[2],
    )


def solution(mesh):
    return jax.shard_map(
        shards,
        mesh=mesh,
        in_specs=(
            P("replica", "shard", None),
            P("replica", "shard", None),
            P("replica", "shard", None),
            P("replica", None),
            P("replica", None),
            P("shard", None),
            P("shard", None),
            P(),
            P(),
            P(),
        ),
        out_specs=(
            P("replica", "shard", None),
            P("replica", "shard", None),
            P("shard", None),
            P("shard", None),
            P(),
            P(),
            P(),
        ),
        check_vma=False,
    )
```

profile of v0, /device:TPU:0, one launch (start us, length us, event | category | flops | bytes accessed | tf_op | source)
XLA Modules:
  0.0 563.7 jit_solution(1563798351276136029)
XLA Ops:
  11.0 4.1 copy.125
  16.2 29.2 %all-gather.8.cloned.1.call-done = bf16[4096,320]{1,0:T(8,128)(2,1)} async-done(((bf16[512,320]{1,0:T(8,128)(2,1)}), bf16[4096,320]{1,0:T(8,128)(2,1)}) %all-gather.8.cloned.1.call-update) | async-done | bytes 2621456 | tf_op jit(solution)/shard_map/all_gather | solution.py:110
  45.4 2.9 fusion.124
  56.4 21.2 %while.194 = (s32[]{:T(128)}, f32[2,64]{1,0:T(2,128)S(1)}, f32[2,64,64,128]{3,2,1,0:T(8,128)}, f32[2,128,64]{2,1,0:T(8,128)S(1)}, f32[2,128,64,1]{1,2,3,0:T(8,12...) while((s32[]{:T(128)}, f32[2,64]{1,0:T(2,128)S(1)}, ...), condition=%wide.region_4.6_spmd, body=%wide.region_2.5_spmd.sunk | while | flops 137928704 | bytes 40800012 | solution.py:117
  63.8 3.1 constant_dynamic-update-slice_fusion.19
  74.4 3.2 constant_dynamic-update-slice_fusion.19
  78.3 7.0 %while.198 = (s32[]{:T(128)}, f32[64]{0:T(128)S(1)}, f32[64,64,128]{2,1,0:T(8,128)}, f32[2,64]{1,0:T(2,128)S(1)}, f32[2,64,64,128]{3,2,1,0:T(8,128)}, /*index=5*/s32[]{:T(128)}, s32[]{:T(128)}) while((s32[]{:T(128)}, f32[64]{0:T(128)S(1)}, f32[64,64,128]{2,1,0:T(8,128)}, f32[2,64]{1,0:T(2,128)S(1)}, f32[2,64,64,128]{3,2,1,0:T(8,128)}, ...), condition=%wide.region_7.9_spmd.clone, body=%wide.region_6.8_spmd.clone.sunk | while | flops 1572995 | bytes 6292832 | solution.py:148
  78.3 3.2 bitcast_add_fusion.13
  81.5 3.8 bitcast_add_fusion.13
  88.3 4.1 convert.12
  93.8 14.1 %all-reduce.5 = bf16[512]{0:T(512)(128)(2,1)S(1)} all-reduce(bf16[512]{0:T(512)(128)(2,1)S(1)} %dynamic-update-slice), channel_id=3, replica_groups=mesh['replica'=4,'shard'=8] {'shard'}, use_global_device_ids=true, to_apply=%add.5 | all-reduce | flops 512 | bytes 2048
  108.0 34.7 %all-gather.10.cloned.1.call-done = bf16[512,64,128]{2,1,0:T(8,128)(2,1)} async-done(((bf16[64,64,128]{2,1,0:T(8,128)(2,1)}), bf16[512,64,128]{2,1,0:T(8,128)(2,1)}) %all-gather.10.cloned.1.call-update) | async-done | bytes 8388624 | tf_op jit(solution)/shard_map/all_gather | solution.py:13
  142.7 27.9 %while.199 = (s32[]{:T(128)}, f32[64,64,128]{2,1,0:T(8,128)}, s32[]{:T(128)}, bf16[8,64,64,128]{3,2,1,0:T(8,128)(2,1)}, bf16[8,64]{1,0:T(8,128)(2,1)S(1)}, /*index=5*/s32[]{:T(128)}, s32[]{:T(128)}) while((s32[]{:T(128)}, f32[64,64,128]{2,1,0:T(8,128)}, s32[]{:T(128)}, bf16[8,64,64,128]{3,2,1,0:T(8,128)(2,1)}, ...), condition=%wide.region_9.11_spmd.clone, body=%wide.region_8.10_spmd.clone.sunk | while | flops 2621508 | bytes 5243625 | solution.py:31
  142.7 2.9 fusion.199
  145.6 3.6 fusion.199
  149.2 3.6 fusion.199
  152.8 3.6 fusion.199
  156.3 3.6 fusion.199
  159.9 3.6 fusion.199
  163.5 3.6 fusion.199
  167.0 3.6 fusion.199
  173.1 15.8 %while.195 = (s32[]{:T(128)}, f32[64,64,128]{2,1,0:T(8,128)}, f32[2,64,64,128]{3,2,1,0:T(8,128)}, f32[2,64]{1,0:T(2,128)S(1)}, f32[2,64,64,128]{3,2,1,0:T(8,128)}, /*index=5*/f32[2]{0:T(128)S(1)}, s32[]{:T(128)}) while((s32[]{:T(128)}, f32[64,64,128]{2,1,0:T(8,128)}, f32[2,64,64,128]{3,2,1,0:T(8,128)}, f32[2,64]{1,0:T(2,128)S(1)}, ...), condition=%wide.region_11.13_spmd, body=%wide.region_10.12_spmd.sunk | while | flops 1572866 | bytes 27264892 | solution.py:155
  173.6 4.1 bitcast_dynamic-update-slice_fusion.23
  177.7 3.2 bitcast_add_fusion.11
  181.6 4.0 bitcast_dynamic-update-slice_fusion.23
  185.6 3.2 bitcast_add_fusion.11
  188.8 4.0 convert.56
  200.9 40.2 %while.197 = (s32[]{:T(128)}, bf16[2,128,128]{2,1,0:T(8,128)(2,1)}, bf16[2,128,128]{2,1,0:T(8,128)(2,1)S(1)}, f32[2,64,128,128]{3,2,1,0:T(8,128)}, f32[2,1,128,1...) while((s32[]{:T(128)}, bf16[2,128,128]{2,1,0:T(8,128)(2,1)}, ...), condition=%wide.region_14.16_spmd.clone, body=%wide.region_12.15_spmd.clone.sunk | while | flops 148373504 | bytes 75078808 | solution.py:128
  202.6 3.9 fusion.195
  222.7 3.9 fusion.195
  246.6 60.3 %while.200 = (s32[]{:T(128)}, f32[64]{0:T(128)}, f32[64]{0:T(128)}, bf16[2,128,256]{2,1,0:T(8,128)(2,1)}, f32[2,128,64]{2,1,0:T(8,128)}, /*index=5*/bf16[2,128,4...) while((s32[]{:T(128)}, f32[64]{0:T(128)}, f32[64]{0:T(128)}, ...), condition=%wide.region_24.26_spmd.clone, body=%wide.region_15.25_spmd.clone.sunk | while | flops 567435520 | bytes 130551072 | solution.py:128
  247.3 3.1 constant_dynamic-slice_fusion.11
  250.4 2.9 copy.169
  262.2 5.0 fusion.212
  277.4 3.1 constant_dynamic-slice_fusion.11
  280.6 2.9 copy.169
  292.3 5.0 fusion.212
  307.0 5.0 broadcast_multiply_fusion
  312.0 7.0 %while.201 = (s32[]{:T(128)}, f32[64]{0:T(128)S(1)}, f32[64,64,128]{2,1,0:T(8,128)}, f32[2,64]{1,0:T(2,128)S(1)}, f32[2,64,64,128]{3,2,1,0:T(8,128)}, /*index=5*/s32[]{:T(128)}, s32[]{:T(128)}) while((s32[]{:T(128)}, f32[64]{0:T(128)S(1)}, f32[64,64,128]{2,1,0:T(8,128)}, f32[2,64]{1,0:T(2,128)S(1)}, ...), condition=%wide.region_26.28_spmd.clone, body=%wide.region_25.27_spmd.clone.sunk | while | flops 1572996 | bytes 6292844 | solution.py:160
  312.0 3.2 bitcast_add_fusion.15
  315.2 3.8 bitcast_add_fusion.15
  322.1 13.2 %all-reduce.6 = bf16[512]{0:T(512)(128)(2,1)S(1)} all-reduce(bf16[512]{0:T(512)(128)(2,1)S(1)} %dynamic-update-slice.1), channel_id=5, replica_groups=mesh['replica'=4,'shard'=8] {'shard'}, use_global_device_ids=true, to_apply=%add.6 | all-reduce | flops 512 | bytes 2048
  335.5 40.8 %all-gather.12.cloned.1.call-done = bf16[512,64,128]{2,1,0:T(8,128)(2,1)} async-done(((bf16[64,64,128]{2,1,0:T(8,128)(2,1)}), bf16[512,64,128]{2,1,0:T(8,128)(2,1)}) %all-gather.12.cloned.1.call-update) | async-done | bytes 8388624 | tf_op jit(solution)/shard_map/all_gather | solution.py:13
  376.2 27.9 %while.202 = (s32[]{:T(128)}, f32[64,64,128]{2,1,0:T(8,128)}, s32[]{:T(128)}, bf16[8,64,64,128]{3,2,1,0:T(8,128)(2,1)}, bf16[8,64]{1,0:T(8,128)(2,1)S(1)}, /*index=5*/s32[]{:T(128)}, s32[]{:T(128)}, s32[]{:T(128)}, s32[]{:T(128)}) while((s32[]{:T(128)}, f32[64,64,128]{2,1,0:T(8,128)}, s32[]{:T(128)}, ...), condition=%wide.region_28.30_spmd.clone, body=%wide.region_27.29_spmd.clone.sunk | while | flops 2621512 | bytes 5243687 | solution.py:31
  376.3 2.9 fusion.219
  379.2 3.6 fusion.219
  382.8 3.6 fusion.219
  386.3 3.6 fusion.219
  389.9 3.6 fusion.219
  393.5 3.6 fusion.219
  397.0 3.6 fusion.219
  400.6 3.6 fusion.219
  406.6 13.1 %while.196 = (s32[]{:T(128)}, f32[64,64,128]{2,1,0:T(8,128)}, f32[2,64,64,128]{3,2,1,0:T(8,128)}, f32[2,64]{1,0:T(2,128)S(1)}, f32[2,64,64,128]{3,2,1,0:T(8,128)}, /*index=5*/s32[]{:T(128)}) while((s32[]{:T(128)}, f32[64,64,128]{2,1,0:T(8,128)}, f32[2,64,64,128]{3,2,1,0:T(8,128)}, f32[2,64]{1,0:T(2,128)S(1)}, ...), condition=%wide.region_30.32_spmd, body=%wide.region_29.31_spmd.sunk | while | flops 1048579 | bytes 27263864 | solution.py:166
  406.6 3.3 bitcast_dynamic-update-slice_fusion.24
  409.9 3.2 bitcast_add_fusion.12
  413.2 3.3 bitcast_dynamic-update-slice_fusion.24
  416.5 3.2 bitcast_add_fusion.12
  419.7 7.0 %fusion.139 = (bf16[2,64,64,128]{3,2,1,0:T(8,128)(2,1)}, f32[2,64]{1,0:T(2,128)S(1)}) fusion(f32[2,64,64,128]{3,2,1,0:T(8,128)} %get-tuple-element.2433, f32[2,64,64,128]{3,2,1,0:T(8,128)} %get-tuple-element.2378), kind=kLoop, calls=%fused_computation.230 | loop fusion | flops 3145600 | bytes 10486272
  429.7 22.4 %while.203 = (s32[]{:T(128)}, f32[64]{0:T(128)S(1)}, bf16[2,128,256]{2,1,0:T(8,128)(2,1)}, f32[2,128,64]{2,1,0:T(8,128)}, bf16[2,128,4096]{1,2,0:T(8,128)(2,1)},...) while((s32[]{:T(128)}, f32[64]{0:T(128)S(1)}, ...), condition=%wide.region_37.39_spmd.clone, body=%wide.region_32.38_spmd.clone.sunk | while | flops 272179392 | bytes 18716728 | solution.py:117
  457.8 43.6 %reduce-scatter.2.cloned.1.call-done = bf16[512,320]{0,1:T(8,128)(2,1)} async-done(((bf16[4096,320]{0,1:T(8,128)(2,1)}), bf16[512,320]{0,1:T(8,128)(2,1)}) %reduce-scatter.2.cloned.1.call-update) | async-done | bytes 327696 | tf_op jit(solution)/shard_map/reduce_scatter | solution.py:179
  501.5 4.1 add.261
  505.5 4.1 copy.133
  509.7 39.5 %all-reduce.7 = (f32[64]{0:T(128)}, f32[64]{0:T(128)}, f32[64]{0:T(128)}) all-reduce(f32[64]{0:T(128)S(1)} %add.266, f32[64]{0:T(128)S(1)} %get-tuple-element.2556, f32[64]{0:T(128)S(1)} %copy-done.40), channel_id=1, replica_groups=mesh['replica'=4,'shard'=8] {'replica','shard'}, use_global_device_ids=true, to_apply=%region_40.42 | all-reduce | flops 192 | bytes 1536 | tf_op jit(solution)/shard_map/psum | solution.py:183
  549.1 4.5 fusion.120
  (422 shorter events, 159.5 us)
Async XLA Ops:
  7.2 38.2 %copy-start = (bf16[1,256,4096]{2,1,0:T(8,128)(2,1)S(1)}, bf16[1,256,4096]{2,1,0:T(8,128)(2,1)}, u32[]{:S(2)}) copy-start(bf16[1,256,4096]{2,1,0:T(8,128)(2,1)} %param.31) | copy-start | bytes 6291460
  7.2 38.2 %all-gather.8.cloned.1.call-start = ((), (), s32[]{:S(2)}) async-start(), calls=%async_computation.1 | async-start | bytes 3538944 | tf_op jit(solution)/shard_map/all_gather | solution.py:110
  10.1 132.6 %all-gather.10.cloned.1.call-start = ((), (), s32[]{:S(2)}) async-start(), calls=%async_computation.4 | async-start | bytes 9437184 | tf_op jit(solution)/shard_map/all_gather | solution.py:13
  11.0 4.1 copy-start.48
  11.0 4.3 copy-start.49
  11.0 4.5 copy-start.50
  16.2 32.1 %copy-start.43 = (f32[256]{0:T(256)}, f32[256]{0:T(256)S(1)}, u32[]{:S(2)}) copy-start(f32[256]{0:T(256)S(1)} %get-tuple-element.2579) | copy-start | bytes 3076
  16.2 32.8 %copy-start.45 = (f32[64]{0:T(128)S(1)}, f32[64]{0:T(128)}, u32[]{:S(2)}) copy-start(f32[64]{0:T(128)} %param.39) | copy-start | bytes 772
  58.8 2.1 copy-start.1
  58.8 3.1 copy-start.17
  69.3 3.1 copy-start.17
  88.1 288.2 %all-gather.12.cloned.1.call-start = ((), (), s32[]{:S(2)}) async-start(), calls=%async_computation.5 | async-start | bytes 9437184 | tf_op jit(solution)/shard_map/all_gather | solution.py:13
  88.3 4.1 copy-start.51
  173.6 4.1 copy-start.4
  181.6 4.0 copy-start.4
  188.8 4.0 copy-start.32
  188.8 4.0 copy-start.44
  206.6 2.9 copy-start.5
  213.9 4.0 copy-start.46
  215.4 2.4 copy-start.14
  215.4 3.1 copy-start.6
  226.7 2.8 copy-start.5
  234.0 4.0 copy-start.46
  235.4 2.4 copy-start.14
  235.4 3.1 copy-start.6
  247.3 10.6 %copy-start.27 = (f32[128]{0:T(128)}, f32[128]{0:T(128)S(1)}, u32[]{:S(2)}) copy-start(f32[128]{0:T(128)S(1)} %fusion.210) | copy-start | bytes 1540 | tf_op jit(solution)/shard_map/transpose(jvp())/while
  254.1 3.8 copy-start.9
  256.1 2.2 copy-start.2
  259.8 2.4 copy-start.16
  259.8 2.4 copy-start.28
  260.0 2.2 copy-start.12
  262.2 5.1 copy-start.7
  262.2 5.9 %copy-start.8 = (f32[2,128,64,64]{1,3,2,0:T(8,128)S(1)}, f32[2,128,64,64]{1,3,2,0:T(8,128)}, u32[]{:S(2)}) copy-start(f32[2,128,64,64]{1,3,2,0:T(8,128)} %get-tuple-element.3553) | copy-start | bytes 12582916 | tf_op jit(solution)/shard_map/transpose(jvp())/while
  271.4 4.2 copy-start.22
  271.4 4.9 copy-start.29
  271.4 4.9 copy-start.30
  271.4 4.9 copy-start.35
  271.4 4.9 copy-start.38
  277.4 10.5 %copy-start.27 = (f32[128]{0:T(128)}, f32[128]{0:T(128)S(1)}, u32[]{:S(2)}) copy-start(f32[128]{0:T(128)S(1)} %fusion.210) | copy-start | bytes 1540 | tf_op jit(solution)/shard_map/transpose(jvp())/while
  284.2 3.7 copy-start.9
  286.2 2.2 copy-start.2
  289.9 2.4 copy-start.16
  289.9 2.4 copy-start.28
  290.1 2.2 copy-start.12
  292.3 5.1 copy-start.7
  292.3 5.9 %copy-start.8 = (f32[2,128,64,64]{1,3,2,0:T(8,128)S(1)}, f32[2,128,64,64]{1,3,2,0:T(8,128)}, u32[]{:S(2)}) copy-start(f32[2,128,64,64]{1,3,2,0:T(8,128)} %get-tuple-element.3553) | copy-start | bytes 12582916 | tf_op jit(solution)/shard_map/transpose(jvp())/while
  301.5 4.2 copy-start.22
  301.5 4.9 copy-start.29
  301.5 4.9 copy-start.30
  301.5 4.9 copy-start.35
  301.5 4.9 copy-start.38
  306.9 5.0 copy-start.33
  306.9 5.0 copy-start.34
  321.8 179.6 %reduce-scatter.2.cloned.1.call-start = ((), (), s32[]{:S(2)}) async-start(), calls=%async_computation.2 | async-start | bytes 2949120 | tf_op jit(solution)/shard_map/reduce_scatter | solution.py:179
  406.6 3.3 copy-start.3
  413.2 3.3 copy-start.3
  426.7 2.9 copy-start.20
  426.7 2.9 copy-start.31
  426.7 2.9 copy-start.42
  436.5 3.7 copy-start.24
  447.8 3.7 copy-start.24
  457.8 95.8 %all-reduce.10.cloned.1.call-start = ((), (), s32[]{:S(2)}) async-start(), calls=%async_computation.3 | async-start | bytes 655360 | tf_op jit(solution)/shard_map/psum | solution.py:182
  505.5 4.1 copy-start.37
  505.5 4.1 copy-start.40
  (24 other events, 25.2 us)
Sparse Core Ops, SparseCore 0:
  10.4 34.8 all-gather.7
  88.2 54.4 all-gather.9
  321.9 54.2 all-gather.11
  457.9 43.4 reduce-scatter.1
  503.6 36.6 all-reduce.9
where the time goes:
time: 566 us; the launch traced here: 564 us
  other arithmetic  171 us (30%)
  waiting for transfers between devices  148 us (26%)
  local copies, waits for them, and re-layouts  112 us (20%)
  blocking collectives  66.8 us (12%)
  matrix products  48.8 us (9%)
  between operations  14.8 us (3%)
    all_gather x2, waiting for transfers between devices, entering_2(): lax.all_gather(part.astype(kind), axis)  75.5 us
    select_n x16, other arithmetic, step(): return jax.tree.map(lambda a, b: jnp.where(reached, a, b), new, before)  55.7 us
    reduce_scatter x1, waiting for transfers between devices, shards(): lax.psum_scatter(grads_local.astype(jnp.bfloat16), 'shard', scatter_dimen...  43.6 us
    psum x1, blocking collectives, shards(): lax.psum((decay_first + decay_second, jnp.sum(raw_cot, axis=0), skip_loca...  39.5 us
    all_gather x1, waiting for transfers between devices, shards(): gathered = lax.all_gather(joined, 'shard', axis=0, tiled=True)  29.2 us
    another operation x21, local copies, waits for them, and re-layouts  28.4 us
    unnamed x2, blocking collectives  27.3 us
    while x124, local copies, waits for them, and re-layouts  19.8 us
  transfers between devices with their start and end apart: 5, of which 4 were waited for; matrix products, arithmetic and copies ran while one was open for 4% of the time, Pallas kernels for 0%

commit v1 on v0

v1 whole, which is shorter than its diff:
```python
import jax
import jax.numpy as jnp
from jax import lax
from jax.experimental import pallas as pl
from jax.experimental.pallas import tpu as pltpu
from jax.sharding import PartitionSpec as P

STATE = 128
SPAN = 128
GROUP = 8
F32, BF16 = jnp.float32, jnp.bfloat16


def span_layout(episode_spans, last_valid, first_span, span_count):
    span_ids = first_span + jnp.arange(span_count, dtype=jnp.int32)
    starts = jnp.cumsum(episode_spans) - episode_spans
    finals = starts + episode_spans - 1
    resets = jnp.any(span_ids[:, None] == starts[None, :], axis=1)
    final_hit = span_ids[:, None] == finals[None, :]
    valid_count = jnp.sum(jnp.where(final_hit, last_valid[None, :] - SPAN, 0), axis=1) + SPAN
    offsets = jnp.arange(SPAN, dtype=jnp.int32)
    valid_mask = jnp.where(offsets[None, :] < valid_count[:, None], 1.0, 0.0).astype(jnp.float32)
    keep_flag = jnp.where(resets, 0.0, 1.0).astype(jnp.float32)
    return (valid_mask, keep_flag)


def dot(a, b, ca, cb):
    return lax.dot_general(a, b, (((ca,), (cb,)), ((), ())), preferred_element_type=F32)


def local_kernel(
    x_ref, g_ref, bc_ref, valid_ref, cols_ref, cum_ref, dt_ref, skip_ref,
    dx_ref, end_ref, dent_ref, rowq_ref, colp_ref, ds_ref, skip_out,
):
    group = pl.program_id(1)
    width = x_ref.shape[1] // GROUP
    b, c = bc_ref[:, :STATE], bc_ref[:, STATE:]
    scores = dot(c, b, 1, 1)
    rows = lax.broadcasted_iota(jnp.int32, (SPAN, SPAN), 0)
    lanes = lax.broadcasted_iota(jnp.int32, (SPAN, SPAN), 1)
    causal = rows >= lanes
    lane8 = lax.broadcasted_iota(jnp.int32, (SPAN, GROUP), 1)
    valid = valid_ref[...]
    rowq = jnp.zeros((SPAN, GROUP), F32)
    ds = jnp.zeros((SPAN, SPAN), F32)
    for pair in range(GROUP // 2):
        at = slice(2 * width * pair, 2 * width * (pair + 1))
        first = lanes < width
        x = x_ref[:, at]
        gf = g_ref[:, at].astype(F32) * valid
        xf = x.astype(F32)

        def spread(which):
            two = cols_ref[which, 0, :, 2 * pair : 2 * pair + 2]
            return jnp.where(first, two[:, 0:1], two[:, 1:2])

        skip_out[0, :, at] = jnp.sum(gf * xf, axis=0, keepdims=True)
        dx = gf * skip_ref[:, at]
        for side in range(2):
            h = 2 * pair + side
            mine = first if side == 0 else jnp.logical_not(first)
            gk = jnp.where(mine, gf, 0.0).astype(BF16)
            dm = dot(gk, x, 1, 1).astype(BF16).astype(F32)
            gaps = cols_ref[0, 0, :, h : h + 1] - cum_ref[h : h + 1, :]
            decay = jnp.exp(jnp.where(causal, gaps, -jnp.inf))
            dt = dt_ref[h : h + 1, :]
            plain = decay * scores
            mixing = (plain * dt).astype(BF16)
            dx = dx + dot(mixing, gk, 0, 0)
            part = dm * plain
            colp_ref[h : h + 1, :] = jnp.sum(part, axis=0, keepdims=True)
            rowq = jnp.where(lane8 == h, jnp.sum(part * dt, axis=1, keepdims=True), rowq)
            ds = ds + dm * decay * dt
        dx_ref[:, at] = dx.astype(BF16)
        end_ref[0, at, :] = dot((xf * spread(2)).astype(BF16), b, 0, 0)
        dent_ref[0, at, :] = dot((gf * spread(1)).astype(BF16), c, 0, 0).astype(BF16)
    rowq_ref[0] = rowq

    @pl.when(group == 0)
    def _():
        ds_ref[0] = ds

    @pl.when(group != 0)
    def _():
        ds_ref[0] = ds_ref[0] + ds


def carried_kernel(
    x_ref, g_ref, bc_ref, valid_ref, cols_ref, enter_ref, ends_ref, dx1_ref,
    dx_ref, dcum_ref, dw_ref, dbc_ref, dcot_ref,
):
    group = pl.program_id(1)
    width = x_ref.shape[1] // GROUP
    b, c = bc_ref[:, :STATE], bc_ref[:, STATE:]
    lanes = lax.broadcasted_iota(jnp.int32, (SPAN, SPAN), 1)
    lane8 = lax.broadcasted_iota(jnp.int32, (SPAN, GROUP), 1)
    first = lanes < width
    valid = valid_ref[...]
    dcum = jnp.zeros((SPAN, GROUP), F32)
    dw = jnp.zeros((SPAN, GROUP), F32)
    db = jnp.zeros((SPAN, STATE), F32)
    dc = jnp.zeros((SPAN, STATE), F32)
    for pair in range(GROUP // 2):
        at = slice(2 * width * pair, 2 * width * (pair + 1))
        gf = g_ref[:, at].astype(F32) * valid
        xf = x_ref[:, at].astype(F32)

        def spread(which):
            two = cols_ref[which, 0, :, 2 * pair : 2 * pair + 2]
            return jnp.where(first, two[:, 0:1], two[:, 1:2])

        enter, ends = enter_ref[0, at, :], ends_ref[0, at, :]
        enter_low, ends_low = enter.astype(BF16), ends.astype(BF16)
        w = spread(2)
        ge = gf * spread(1)
        moved = dot(c, enter_low, 1, 1) * ge
        back = dot(b, ends_low, 1, 1).astype(BF16).astype(F32)
        xr = xf * back
        dx_ref[:, at] = (dx1_ref[:, at].astype(F32) + w * back).astype(BF16)
        db = db + dot((xf * w).astype(BF16), ends_low, 1, 0)
        dc = dc + dot(ge.astype(BF16), enter_low, 1, 0)
        prod = enter * ends
        for side in range(2):
            h = 2 * pair + side
            mine = first if side == 0 else jnp.logical_not(first)
            dcum = jnp.where(
                lane8 == h, jnp.sum(jnp.where(mine, moved, 0.0), axis=1, keepdims=True), dcum
            )
            dw = jnp.where(
                lane8 == h, jnp.sum(jnp.where(mine, xr, 0.0), axis=1, keepdims=True), dw
            )
            dcot_ref[0, h : h + 1, :] = jnp.sum(
                prod[side * width : (side + 1) * width], axis=0, keepdims=True
            )
    dcum_ref[0] = dcum
    dw_ref[0] = dw

    @pl.when(group == 0)
    def _():
        dbc_ref[:, :STATE] = db
        dbc_ref[:, STATE:] = dc

    @pl.when(group != 0)
    def _():
        dbc_ref[:, :STATE] = dbc_ref[:, :STATE] + db
        dbc_ref[:, STATE:] = dbc_ref[:, STATE:] + dc


def exchange(forward, backward, factor, width):
    count = lax.axis_size("shard")
    heads = factor.shape[0]
    here = heads // count
    factors = lax.all_gather(factor, "shard")
    both = jnp.stack([forward, backward]).astype(BF16)
    both = both.reshape(2, count, here * width, STATE)
    parts = lax.all_to_all(both, "shard", 1, 1, tiled=True).astype(F32)
    mine = lax.dynamic_slice_in_dim(factors, lax.axis_index("shard") * here, here, 1)
    mine = jnp.repeat(mine, width, axis=1)[:, :, None]
    before, after = [jnp.zeros(parts.shape[2:], F32)], [jnp.zeros(parts.shape[2:], F32)]
    for k in range(count - 1):
        before.append(before[-1] * mine[k] + parts[0, k])
        at = count - 1 - k
        after.append(after[-1] * mine[at] + parts[1, at])
    sent = jnp.stack([jnp.stack(before), jnp.stack(after[::-1])]).astype(BF16)
    got = lax.all_to_all(sent, "shard", 1, 1, tiled=True)
    got = got.reshape(2, heads * width, STATE).astype(F32)
    return got[0], got[1]


def shards(
    activations,
    head_inputs,
    out_cotangent,
    episode_spans,
    last_valid,
    mixer_weight,
    step_weight,
    decay_log,
    step_bias,
    skip_gain,
):
    token_rows = activations[0]
    inputs_here = head_inputs[0]
    cot_here = out_cotangent[0]
    tokens, features = inputs_here.shape
    span_count = tokens // SPAN
    heads = decay_log.shape[0]
    width = features // heads
    groups = heads // GROUP
    block = GROUP * width
    first_span = lax.axis_index("shard") * span_count
    valid_mask, keep_flag = span_layout(episode_spans[0], last_valid[0], first_span, span_count)
    valid = valid_mask.reshape(-1, 1)
    joined = jnp.concatenate([mixer_weight, step_weight], axis=1)
    gathered = lax.all_gather(joined, "shard", axis=0, tiled=True)
    projected = jnp.dot(token_rows, gathered, preferred_element_type=F32)
    mixers = projected[:, : 2 * STATE].astype(BF16)
    raw_steps = projected[:, 2 * STATE :] + step_bias[None, :]
    steps = jax.nn.softplus(raw_steps) * valid
    rate = -jnp.exp(decay_log)
    spans = lambda a: a.reshape(span_count, SPAN, heads)
    cum = jnp.cumsum(spans(steps * rate[None, :]), axis=1)
    last = cum[:, -1]
    tail = jnp.exp(last[:, None] - cum)
    weights = tail * spans(steps)
    decays = jnp.exp(last)
    cols = jnp.stack([cum, jnp.exp(cum), weights]).reshape(3, tokens, groups, GROUP)
    cols = cols.transpose(0, 2, 1, 3)
    cum_rows = cum.reshape(tokens, heads).T
    step_rows = steps.T
    skip_wide = jnp.repeat(skip_gain, width)[None]

    wide = pl.BlockSpec((SPAN, block), lambda s, g: (s, g))
    state = pl.BlockSpec((1, block, STATE), lambda s, g: (s, g, 0))
    mix = pl.BlockSpec((SPAN, 2 * STATE), lambda s, g: (s, 0))
    one = pl.BlockSpec((SPAN, 1), lambda s, g: (s, 0))
    three = pl.BlockSpec((3, 1, SPAN, GROUP), lambda s, g: (0, g, s, 0))
    col = pl.BlockSpec((1, SPAN, GROUP), lambda s, g: (g, s, 0))
    row = pl.BlockSpec((GROUP, SPAN), lambda s, g: (g, s))
    shape = jax.ShapeDtypeStruct
    dx1, ends, dent, rowq, colp, ds, skip_rows = pl.pallas_call(
        local_kernel,
        grid=(span_count, groups),
        in_specs=[wide, wide, mix, one, three, row, row, pl.BlockSpec((1, block), lambda s, g: (0, g))],
        out_specs=[
            wide, state, state, col, row,
            pl.BlockSpec((1, SPAN, SPAN), lambda s, g: (s, 0, 0)),
            pl.BlockSpec((1, 1, block), lambda s, g: (s, 0, g)),
        ],
        out_shape=[
            shape((tokens, features), BF16),
            shape((span_count, features, STATE), F32),
            shape((span_count, features, STATE), BF16),
            shape((groups, tokens, GROUP), F32),
            shape((heads, tokens), F32),
            shape((span_count, SPAN, SPAN), F32),
            shape((span_count, 1, features), F32),
        ],
        name="local",
    )(inputs_here, cot_here, mixers, valid, cols, cum_rows, step_rows, skip_wide)

    factors = decays * keep_flag[:, None]
    factor_wide = jnp.repeat(factors, width, axis=1)[:, :, None]
    dent = dent.astype(F32) * keep_flag[:, None, None]
    total, back_total = ends[0], dent[-1]
    product = factors[0]
    for s in range(1, span_count):
        total = total * factor_wide[s] + ends[s]
        r = span_count - 1 - s
        back_total = back_total * factor_wide[r] + dent[r]
        product = product * factors[s]
    before, after = exchange(total, back_total, product, width)
    entering, ends_grad = [], [None] * span_count
    for s in range(span_count):
        entering.append(before * keep_flag[s])
        before = before * factor_wide[s] + ends[s]
        r = span_count - 1 - s
        ends_grad[r] = after
        after = after * factor_wide[r] + dent[r]
    entering, ends_grad = jnp.stack(entering), jnp.stack(ends_grad)

    input_grad, dcum_out, dw, dbc, dcot = pl.pallas_call(
        carried_kernel,
        grid=(span_count, groups),
        in_specs=[wide, wide, mix, one, three, state, state, wide],
        out_specs=[
            wide, col, col, mix,
            pl.BlockSpec((1, GROUP, STATE), lambda s, g: (s, g, 0)),
        ],
        out_shape=[
            shape((tokens, features), BF16),
            shape((groups, tokens, GROUP), F32),
            shape((groups, tokens, GROUP), F32),
            shape((tokens, 2 * STATE), F32),
            shape((span_count, heads, STATE), F32),
        ],
        name="carried",
    )(inputs_here, cot_here, mixers, valid, cols, entering, ends_grad, dx1)

    flat = lambda a: spans(a.transpose(1, 0, 2).reshape(tokens, heads))
    colp = spans(colp.T)
    dw = flat(dw)
    step_spans = spans(steps)
    dww = dw * weights
    dcum = flat(rowq) - colp * step_spans + flat(dcum_out) - dww
    dlast = jnp.sum(dww, axis=1) + jnp.sum(dcot, axis=-1) * decays
    summed_cum = lax.cumsum(dcum, axis=1, reverse=True) + dlast[:, None]
    dstep = colp + dw * tail + summed_cum * rate
    raw_cot = dstep.reshape(tokens, heads) * valid * jax.nn.sigmoid(raw_steps)
    decay_local = jnp.sum(summed_cum * step_spans, axis=(0, 1)) * rate
    skip_local = jnp.sum(skip_rows.reshape(span_count, heads, width), axis=(0, 2))
    small = lax.psum(
        (decay_local, jnp.sum(raw_cot, axis=0), skip_local), ("replica", "shard")
    )
    mixer_spans = mixers.reshape(span_count, SPAN, 2 * STATE)
    ds_low = ds.astype(BF16)
    db = jnp.einsum("cts,ctn->csn", ds_low, mixer_spans[:, :, STATE:], preferred_element_type=F32)
    dc = jnp.einsum("cts,csn->ctn", ds_low, mixer_spans[:, :, :STATE], preferred_element_type=F32)
    mixer_cot = (dbc + jnp.concatenate([db, dc], axis=2).reshape(tokens, 2 * STATE)).astype(BF16)
    joined_cot = jnp.concatenate([mixer_cot, raw_cot.astype(BF16)], axis=1)
    grads_local = dot(token_rows, joined_cot, 0, 0)
    count = lax.axis_size("shard")
    parts = grads_local.astype(BF16).reshape(count, -1, joined_cot.shape[1])
    parts = lax.all_to_all(parts, "shard", 0, 0, tiled=True)
    shared = jnp.sum(parts.astype(F32), axis=0).astype(BF16)
    summed = jnp.sum(lax.all_gather(shared, "replica").astype(F32), axis=0)
    back_rows = dot(joined_cot, gathered, 1, 1)
    return (
        input_grad[None],
        back_rows.astype(BF16)[None],
        summed[:, : 2 * STATE],
        summed[:, 2 * STATE :],
        small[0],
        small[1],
        small[2],
    )


def solution(mesh):
    return jax.shard_map(
        shards,
        mesh=mesh,
        in_specs=(
            P("replica", "shard", None),
            P("replica", "shard", None),
            P("replica", "shard", None),
            P("replica", None),
            P("replica", None),
            P("shard", None),
            P("shard", None),
            P(),
            P(),
            P(),
        ),
        out_specs=(
            P("replica", "shard", None),
            P("replica", "shard", None),
            P("shard", None),
            P("shard", None),
            P(),
            P(),
            P(),
        ),
        check_vma=False,
    )
```

time: 566 us -> 314 us (0.55)
  other arithmetic: 171 us -> 33.2 us
  waiting for transfers between devices: 148 us -> 49.6 us
  local copies, waits for them, and re-layouts: 112 us -> 31 us
  Pallas kernels: 0 us -> 57.4 us
  blocking collectives: 66.8 us -> 106 us
  matrix products: 48.8 us -> 10.8 us
  starting transfers between devices: 0.21 us -> 9.13 us
    all_gather x2 -> x1, waiting for transfers between devices: 75.5 us -> 0.01 us  [shards(): summed = jnp.sum(lax.all_gather(shared, 'replica').astype(F32), axis=0)]
    pallas_call x0 -> x2, Pallas kernels: none -> 57.4 us  [the longest x1 35.9 us: shards(): pl.pallas_call(local_kernel, grid=(span_count, groups), in_specs=[wide, w...]
    select_n x16 -> x0, other arithmetic: 55.7 us -> none  [step(): return jax.tree.map(lambda a, b: jnp.where(reached, a, b), new, before)]
    reduce_scatter x1 -> x0, waiting for transfers between devices: 43.6 us -> none  [shards(): lax.psum_scatter(grads_local.astype(jnp.bfloat16), 'shard', scatter_dimen...]
    dot_general x25 -> x5, matrix products: 48.8 us -> 10.8 us  [the longest x2 5.37 us: dot(): lax.dot_general(a, b, (((ca,), (cb,)), ((), ())), preferred_element_type=...]
    all_to_all x0 -> x1, blocking collectives: none -> 35.4 us  [shards(): parts = lax.all_to_all(parts, 'shard', 0, 0, tiled=True)]
    add x11 -> x3, other arithmetic: 32.1 us -> 0.72 us  [the longest x1 0.69 us: shards(): after = after * factor_wide[r] + dent[r]]
    dynamic_update_slice x18 -> x0, other arithmetic: 31.3 us -> none  [the longest x12 17.9 us: end_part(): lax.map(lambda pieces: span_end(pieces[0], pieces[1], pieces[2], decay_lo...]
  transfers between devices with their start and end apart: 5 -> 4, of which waited for: 4 -> 2; matrix products, arithmetic and copies ran while one was open for 4% -> 6% of each run, Pallas kernels for 0% -> 0%
where the time goes in v1:
time: 314 us; the launch traced here: 312 us
  blocking collectives  106 us (34%)
  Pallas kernels  57.4 us (18%)
  waiting for transfers between devices  49.6 us (16%)
  other arithmetic  33.2 us (11%)
  local copies, waits for them, and re-layouts  31 us (10%)
  between operations  14.6 us (5%)
  matrix products  10.8 us (3%)
  starting transfers between devices  9.13 us (3%)
    psum x1, blocking collectives, shards(): lax.psum((decay_local, jnp.sum(raw_cot, axis=0), skip_local), ('replica',...  41.4 us
    pallas_call x1, Pallas kernels, shards(): pl.pallas_call(local_kernel, grid=(span_count, groups), in_specs=[wide, w...  35.9 us
    all_to_all x1, blocking collectives, shards(): parts = lax.all_to_all(parts, 'shard', 0, 0, tiled=True)  35.4 us
    all_gather x1, waiting for transfers between devices, shards(): gathered = lax.all_gather(joined, 'shard', axis=0, tiled=True)  29.8 us
    all_gather x1, blocking collectives, exchange(): factors = lax.all_gather(factor, 'shard')  29.5 us
    pallas_call x1, Pallas kernels, shards(): pl.pallas_call(carried_kernel, grid=(span_count, groups), in_specs=[wide,...  21.4 us
    all_to_all x1, waiting for transfers between devices, exchange(): got = lax.all_to_all(sent, 'shard', 1, 1, tiled=True)  19.8 us
  transfers between devices with their start and end apart: 4, of which 2 were waited for; matrix products, arithmetic and copies ran while one was open for 6% of the time, Pallas kernels for 0%

profile of v1, /device:TPU:0, one launch (start us, length us, event | category | flops | bytes accessed | tf_op | source)
XLA Modules:
  0.0 312.0 jit_solution(15121011119881586771)
XLA Ops:
  7.2 1.1 copy.101
  8.3 1.7 pad_maximum_fusion.4
  10.1 0.7 broadcast_in_dim.85
  10.8 0.7 broadcast_in_dim_reshape.2.skip_ref
  11.5 0.8 reduce-window.4
  12.3 0.7 add_bitcast_fusion
  13.3 0.8 copy.126.valid_ref
  14.1 0.7 fusion.57
  14.9 0.7 exponential_negate_fusion
  15.6 29.8 %all-gather.5.cloned.1.call-done = bf16[4096,320]{1,0:T(8,128)(2,1)} async-done(((bf16[512,320]{1,0:T(8,128)(2,1)}), bf16[4096,320]{1,0:T(8,128)(2,1)}) %all-gather.5.cloned.1.call-update) | async-done | bytes 2621456 | tf_op jit(solution)/shard_map/all_gather | solution.py:195
  45.4 3.2 %fusion.5 = f32[256,320]{1,0:T(8,128)S(1)} fusion(bf16[4096,320]{1,0:T(8,128)(2,1)} %all-gather.5.cloned.1.call-done, bf16[1,256,4096]{2,1,0:T(8,128)(2,1)S(1)} %copy-done), kind=kOutput, calls=%fused_computation.17 | convolution fusion | flops 671088640 | bytes 5046272 | tf_op jit(solution)/shard_map/dot_general | solution.py:196
  48.6 0.7 slice.355.bc_ref
  49.9 0.3 copy-done.11
  50.8 0.7 copy.109.dt_ref
  51.5 0.7 copy.108.cum_ref
  52.3 2.2 copy.106
  54.6 35.9 %local.1 = (bf16[256,4096]{1,0:T(8,128)(2,1)}, f32[2,4096,128]{2,1,0:T(8,128)}, bf16[2,4096,128]{2,1,0:T(8,128)(2,1)}, f32[8,256,8]{2,1,0:T(8,128)}, f32[64,256]...) custom-call(bf16[256,4096]{1,0:T(8,128)(2,1)} %bitcast.276, bf16[256,4096]{1,0:T(8,128)(2,1)} %bitcast.278, ...), custom_call_target="tpu_custom_call" | custom-call | tf_op jit(solution)/shard_map/local/pallas_call | solution.py:221
  90.5 2.1 convert_multiply_fusion
  92.6 0.7 copy-done.3
  93.3 0.7 add_convert_fusion
  94.0 0.6 copy-done.1
  94.6 0.7 fusion.1
  95.3 1.5 pad_maximum_fusion.2
  96.8 4.4 %all-to-all-start = ((bf16[2,8,512,128]{3,2,0,1:T(8,128)(2,1)}), bf16[2,8,512,128]{3,2,0,1:T(8,128)(2,1)}, u32[]{:S(2)}, u32[]{:S(2)}) async-start(bf16[2,8,512,128]{3,2,0,1:T(8,128)(2,1)} %pad_maximum_fusion.2), calls=%async_computation | async-start | bytes 4194304 | tf_op jit(solution)/shard_map/all_to_all | solution.py:156
  101.2 29.5 %all-gather.1 = f32[8,1,64]{2,1,0:T(1,128)S(1)} all-gather(f32[1,1,64]{2,1,0:T(1,128)S(1)} %get-tuple-element.99), channel_id=1, replica_groups=mesh['replica'=4,'shard'=8] {'shard'}, dimensions={0}, use_global_device_ids=true | all-gather | bytes 2304 | tf_op jit(solution)/shard_map/all_gather | solution.py:153
  132.0 2.0 convert_element_type.38
  134.2 0.2 convert_dynamic-update-slice_fusion.9
  134.6 0.3 convert_dynamic-update-slice_fusion.7
  135.0 0.6 convert_dynamic-update-slice_fusion.5
  135.9 0.3 fusion.29
  136.4 0.2 pad_maximum_fusion.3
  136.6 1.5 copy.125
  138.1 4.5 %all-to-all-start.1 = ((bf16[2,8,512,128]{3,2,0,1:T(8,128)(2,1)}), bf16[2,8,512,128]{3,2,0,1:T(8,128)(2,1)}, u32[]{:S(2)}, u32[]{:S(2)}) async-start(bf16[2,8,512,128]{3,2,0,1:T(8,128)(2,1)} %copy.125), calls=%async_computation.1 | async-start | bytes 4194304 | tf_op jit(solution)/shard_map/all_to_all | solution.py:165
  142.6 0.2 all-gather.7.cloned.1.call-start
  142.8 1.3 fusion.73
  144.2 0.9 copy.133
  145.1 0.9 reshape_reshape.12
  146.1 0.9 copy.130
  147.0 1.1 fusion.39
  148.1 1.1 fusion.41
  149.4 19.8 %all-to-all-done.1 = bf16[2,8,512,128]{3,2,0,1:T(8,128)(2,1)} async-done(((bf16[2,8,512,128]{3,2,0,1:T(8,128)(2,1)}), bf16[2,8,512,128]{3,2,0,1:T(8,128)(2,1)}, u32[]{:S(2)}, u32[]{:S(2)}) %all-to-all-start.1) | async-done | bytes 2097184 | tf_op jit(solution)/shard_map/all_to_all | solution.py:165
  169.2 2.1 fusion.71
  171.4 0.7 copy-done.2
  172.1 0.7 multiply_add_fusion
  172.8 1.5 copy-done.4
  174.2 2.0 broadcast_multiply_fusion
  176.3 3.8 %pad_maximum_fusion = (f32[2,4096,128]{2,1,0:T(8,128)}, f32[2,4096,128]{2,1,0:T(8,128)}) fusion(f32[1,4096,128]{2,1,0:T(8,128)S(1)} %get-tuple-element.85, f32[1,4096,128]{2,1,0:T(8,128)S(1)} %get-tuple-element.84, f32[1,4096,128]{2,1,0:T(8,128)S(1)} %bitcast.273, f32[1,4096,128]{2,1,0:T(8,128)S(1)} %multiply_add_fusion), kind=kLoop, calls=%fused_computation.3 | loop fusion | flops 2097152 | bytes 16777216 | tf_op jit(solution)/shard_map/stack | solution.py:260
  180.1 21.4 %carried.1 = (bf16[256,4096]{1,0:T(8,128)(2,1)}, f32[8,256,8]{2,1,0:T(8,128)}, f32[8,256,8]{2,1,0:T(8,128)}, f32[256,256]{1,0:T(8,128)}, f32[2,64,128]{2,1,0:T(8,128)}) custom-call(bf16[256,4096]{1,0:T(8,128)(2,1)} %bitcast.277, bf16[256,4096]{1,0:T(8,128)(2,1)} %bitcast.279, bf16[256,256]{1,0:T(8,128)(2,1)} %slice.355.bc_ref, f32[256,1]{1,0:T(8,128)} %copy.126.valid_ref, ...), custom_call_target="tpu_custom_call" | custom-call | tf_op jit(solution)/shard_map/carried/pallas_call | solution.py:262
  201.5 0.9 reduce_sum.89
  202.5 1.5 copy.131
  204.2 1.5 copy.135
  205.9 2.2 reduce_window_sum.29
  208.2 1.0 fusion.24
  209.3 1.0 fusion.62
  210.3 0.9 convolution_convert_fusion
  211.2 0.2 copy.165
  211.4 35.4 %all_to_all.15 = bf16[8,512,320]{1,2,0:T(8,128)(2,1)} all-to-all(bf16[8,512,320]{1,2,0:T(8,128)(2,1)S(1)} %bitcast.275), channel_id=1, replica_groups=mesh['replica'=4,'shard'=8] {'shard'}, dimensions={0} | all-to-all | bytes 5242880 | tf_op jit(solution)/shard_map/all_to_all | solution.py:304
  246.8 2.9 reduce_sum.91
  250.0 41.4 %all-reduce = (f32[64]{0:T(128)}, f32[64]{0:T(128)}, f32[64]{0:T(128)}) all-reduce(f32[64]{0:T(128)S(1)} %fusion.61, f32[64]{0:T(128)S(1)} %get-tuple-element.62, f32[64]{0:T(128)S(1)} %reduce_sum.97), channel_id=1, replica_groups=mesh['replica'=4,'shard'=8] {'replica','shard'}, use_global_device_ids=true, to_apply=%region_10.11 | all-reduce | flops 192 | bytes 1536 | tf_op jit(solution)/shard_map/psum | solution.py:292
  291.5 4.5 %fusion = bf16[1,256,4096]{2,1,0:T(8,128)(2,1)} fusion(bf16[4096,320]{1,0:T(8,128)(2,1)} %all-gather.5.cloned.1.call-done, bf16[256,64]{1,0:T(8,128)(2,1)S(1)} %get-tuple-element.63, bf16[256,256]{1,0:T(8,128)(2,1)S(1)} %fusion.24), kind=kOutput, calls=%fused_computation.2 | convolution fusion | flops 672464896 | bytes 4882432 | tf_op jit(solution)/shard_map/dot_general | solution.py:28
  296.0 4.2 %reshape.2014 = f32[4,512,320]{1,0,2:T(4,128)} reshape(bf16[2048,320]{0,1:T(8,128)(2,1)} %all-gather.7.cloned.1.call-done) | data formatting | bytes 3932160 | tf_op jit(solution)/shard_map/convert_element_type | solution.py:306
  300.2 3.3 %reduce_sum.92 = f32[512,320]{0,1:T(8,128)S(1)} reduce(f32[4,512,320]{1,0,2:T(4,128)} %reshape.2014, f32[]{:T(128)} %constant.21.clone.1), dimensions={0}, to_apply=%region_8.9 | reduce | flops 491520 | bytes 3276804 | tf_op jit(solution)/shard_map/reduce_sum | solution.py:306
  303.5 0.7 slice.253
  304.2 1.0 copy.143
  (109 shorter events, 5.0 us)
Async XLA Ops:
  7.2 38.2 %copy-start = (bf16[1,256,4096]{2,1,0:T(8,128)(2,1)S(1)}, bf16[1,256,4096]{2,1,0:T(8,128)(2,1)}, u32[]{:S(2)}) copy-start(bf16[1,256,4096]{2,1,0:T(8,128)(2,1)} %param.10) | copy-start | bytes 6291460
  7.2 38.2 %all-gather.5.cloned.1.call-start = ((), (), s32[]{:S(2)}) async-start(), calls=%async_computation.3 | async-start | bytes 3538944 | tf_op jit(solution)/shard_map/all_gather | solution.py:195
  13.3 36.0 %copy-start.13 = (f32[256]{0:T(256)}, f32[256]{0:T(256)S(1)}, u32[]{:S(2)}) copy-start(f32[256]{0:T(256)S(1)} %get-tuple-element.104) | copy-start | bytes 3076
  15.6 33.7 %copy-start.18 = (f32[64]{0:T(128)}, f32[64]{0:T(128)S(1)}, u32[]{:S(2)}) copy-start(f32[64]{0:T(128)S(1)} %exponential_negate_fusion) | copy-start | bytes 772
  15.6 74.9 %copy-start.15 = (f32[2]{0:T(128)}, f32[2]{0:T(128)S(1)}, u32[]{:S(2)}) copy-start(f32[2]{0:T(128)S(1)} %broadcast_select_fusion) | copy-start | bytes 28
  15.6 33.7 %copy-start.16 = (f32[64]{0:T(128)S(1)}, f32[64]{0:T(128)}, u32[]{:S(2)}) copy-start(f32[64]{0:T(128)} %param.18) | copy-start | bytes 772
  48.6 0.9 copy-start.7
  49.6 0.6 copy-start.11
  50.4 42.3 %copy-start.8 = (f32[4096]{0:T(1024)}, f32[4096]{0:T(1024)S(1)}, u32[]{:S(2)}) copy-start(f32[4096]{0:T(1024)S(1)} %broadcast_in_dim.87) | copy-start | bytes 49156
  90.5 2.8 copy-start.3
  92.6 2.0 copy-start.1
  96.8 35.2 %all-to-all-start = ((bf16[2,8,512,128]{3,2,0,1:T(8,128)(2,1)}), bf16[2,8,512,128]{3,2,0,1:T(8,128)(2,1)}, u32[]{:S(2)}, u32[]{:S(2)}) async-start(bf16[2,8,512,128]{3,2,0,1:T(8,128)(2,1)} %pad_maximum_fusion.2), calls=%async_computation | async-start | bytes 4194304 | tf_op jit(solution)/shard_map/all_to_all | solution.py:156
  138.1 6.1 %copy-start.6 = (f32[8,256,8]{2,1,0:T(8,128)S(1)}, f32[8,256,8]{2,1,0:T(8,128)}, u32[]{:S(2)}) copy-start(f32[8,256,8]{2,1,0:T(8,128)} %get-tuple-element.27) | copy-start | bytes 196612
  138.1 8.9 %copy-start.5 = (bf16[256,256]{1,0:T(8,128)(2,1)S(1)}, bf16[256,256]{1,0:T(8,128)(2,1)}, u32[]{:S(2)}) copy-start(bf16[256,256]{1,0:T(8,128)(2,1)} %slice.355.bc_ref) | copy-start | bytes 393220
  138.1 31.1 %all-to-all-start.1 = ((bf16[2,8,512,128]{3,2,0,1:T(8,128)(2,1)}), bf16[2,8,512,128]{3,2,0,1:T(8,128)(2,1)}, u32[]{:S(2)}, u32[]{:S(2)}) async-start(bf16[2,8,512,128]{3,2,0,1:T(8,128)(2,1)} %copy.125), calls=%async_computation.1 | async-start | bytes 4194304 | tf_op jit(solution)/shard_map/all_to_all | solution.py:165
  142.6 153.4 %all-gather.7.cloned.1.call-start = ((), (), s32[]{:S(2)}) async-start(), calls=%async_computation.4 | async-start | bytes 1638400 | tf_op jit(solution)/shard_map/all_gather | solution.py:306
  149.4 22.0 %copy-start.9 = (f32[4096]{0:T(1024)S(1)}, f32[4096]{0:T(1024)}, u32[]{:S(2)}) copy-start(f32[4096]{0:T(1024)} %copy-done.8) | copy-start | bytes 49156
  169.2 2.8 copy-start.2
  172.1 2.2 copy-start.4
  201.5 4.3 %copy-start.12 = (f32[2,1,64]{2,1,0:T(1,128)S(1)}, f32[2,1,64]{2,1,0:T(1,128)}, u32[]{:S(2)}) copy-start(f32[2,1,64]{2,1,0:T(1,128)} %copy-done.11) | copy-start | bytes 1540
  204.0 5.3 %copy-start.14 = (f32[256]{0:T(256)S(1)}, f32[256]{0:T(256)}, u32[]{:S(2)}) copy-start(f32[256]{0:T(256)} %copy-done.13) | copy-start | bytes 3076
  204.0 5.3 %copy-start.17 = (f32[64]{0:T(128)S(1)}, f32[64]{0:T(128)}, u32[]{:S(2)}) copy-start(f32[64]{0:T(128)} %param.18) | copy-start | bytes 772
  204.0 5.3 %copy-start.19 = (f32[64]{0:T(128)S(1)}, f32[64]{0:T(128)}, u32[]{:S(2)}) copy-start(f32[64]{0:T(128)} %copy-done.18) | copy-start | bytes 772
  246.8 3.0 copy-start.10
  246.8 3.2 %copy-start.20 = (f32[64]{0:T(128)S(1)}, f32[64]{0:T(128)}, u32[]{:S(2)}) copy-start(f32[64]{0:T(128)} %param.17) | copy-start | bytes 772
Sparse Core Ops, SparseCore 0:
  10.4 34.8 all-gather.4
  249.9 32.5 all-gather.6
